TPU v7x, 32 devices: a whole 2x2x4 slice. The times are simulated.
32 devices in a mesh: segment: 4 (over y, x), seq: 8 (over z, core).
Axes of the slice: x: 2, y: 2, z: 4, core: 2. Of those that a mesh axis runs over, the one named last changes fastest.
Arguments:
- hidden: bfloat16 [4, 8192, 8192], P('segment', 'seq'), may hold values from -6 to 6
- span_lengths: int32 [4, 64], replicated, may hold values from 1 to 512, 8192 in all within a row
- section_of: int32 [4, 64], replicated, may hold values from 0 to 31
- section_live: int32 [32], P('seq'), may hold values 0 or 1
- w_in: bfloat16 [8192, 2048], P('seq'), may hold values from -0.5 to 0.5
- norm_gain: float32 [2048], replicated, may hold values from 0.5 to 1.5
- w_query: bfloat16 [2048, 2048], P(None, 'segment'), may hold values from -0.125 to 0.125
- w_key: bfloat16 [2048, 2048], P(None, 'segment'), may hold values from -0.125 to 0.125
- w_value: bfloat16 [2048, 2048], P(None, 'segment'), may hold values from -0.125 to 0.125
- w_out: bfloat16 [2048, 2048], P('segment'), may hold values from -0.125 to 0.125
Outputs:
- section_out: bfloat16 [32, 2048], P('seq')
All inputs are finite; a program needn't handle non-finite values. No bound on the sum of `section_live` on one device may be relied on, other than what follows from the above.
Results may differ from a plain program's by a relative error of at most 0.007.
Values may be sent and summed in bfloat16 or wider, within the bound.
A program may use at most 128 MiB of HBM per device.

v0:
```python
import jax
import jax.numpy as jnp
from jax import lax
from jax.sharding import PartitionSpec as P

HEAD_DIM = 128


def shards(
    hidden, span_lengths, section_of, section_live, w_in, norm_gain, w_query, w_key, w_value, w_out
):
    tokens = hidden[0]
    seq_count = lax.axis_size("seq")
    seq_index = lax.axis_index("seq")
    segment_index = lax.axis_index("segment")
    tok_count = tokens.shape[0]
    lengths = lax.dynamic_index_in_dim(span_lengths, segment_index, 0, keepdims=False)
    span_ends = jnp.cumsum(lengths)
    span_starts = span_ends - lengths
    positions = seq_index * tok_count + jnp.arange(tok_count, dtype=jnp.int32)
    member = (
        (positions[None, :] >= span_starts[:, None]) & (positions[None, :] < span_ends[:, None])
    ).astype(jnp.bfloat16)
    partial_value = jnp.dot(member, tokens, preferred_element_type=jnp.float32)
    length_float = lengths.astype(jnp.float32)
    sections_here = section_live.shape[0]
    section_total = sections_here * seq_count
    section_ids = jnp.arange(section_total, dtype=jnp.int32)
    own_sections = seq_index * sections_here + jnp.arange(sections_here, dtype=jnp.int32)
    flat_sections = section_of.reshape(-1)
    count_all = jnp.sum(
        (section_ids[:, None] == flat_sections[None, :]).astype(jnp.float32), axis=1
    )
    doc_sections = lax.dynamic_index_in_dim(section_of, segment_index, 0, keepdims=False)
    weighted = partial_value / length_float[:, None]
    doc_onehot = (section_ids[:, None] == doc_sections[None, :]).astype(jnp.float32)
    section_part = jnp.dot(doc_onehot, weighted, precision=lax.Precision.HIGHEST)
    feature_block = lax.psum_scatter(section_part, "seq", scatter_dimension=1, tiled=True)
    doc_total = lax.psum(feature_block, "segment")
    pooled = (doc_total / jnp.maximum(count_all, 1.0)[:, None]).astype(jnp.bfloat16)
    projected = jnp.dot(pooled, w_in, preferred_element_type=jnp.float32)
    section_in = lax.psum_scatter(projected, "seq", scatter_dimension=0, tiled=True)
    scale = lax.rsqrt(jnp.mean(section_in * section_in, axis=1, keepdims=True) + 1e-05)
    normed = (section_in * scale * norm_gain[None, :]).astype(jnp.bfloat16)
    queries = jnp.dot(normed, w_query, preferred_element_type=jnp.float32).astype(jnp.bfloat16)
    keys_here = jnp.dot(normed, w_key, preferred_element_type=jnp.float32).astype(jnp.bfloat16)
    values_here = jnp.dot(normed, w_value, preferred_element_type=jnp.float32).astype(jnp.bfloat16)
    live_here = section_live.astype(jnp.bfloat16)
    keys_all, values_all, live_all = (
        lax.all_gather(keys_here, "seq", axis=0, tiled=True),
        lax.all_gather(values_here, "seq", axis=0, tiled=True),
        lax.all_gather(live_here, "seq", axis=0, tiled=True),
    )
    local_heads = queries.shape[1] // HEAD_DIM
    query_heads = queries.reshape(sections_here, local_heads, HEAD_DIM)
    key_heads = keys_all.reshape(section_total, local_heads, HEAD_DIM)
    value_heads = values_all.reshape(section_total, local_heads, HEAD_DIM)
    scores = jnp.einsum("qhd,khd->hqk", query_heads, key_heads, preferred_element_type=jnp.float32)
    scores = scores / jnp.sqrt(jnp.float32(HEAD_DIM))
    allowed = (live_all[None, :] > 0) | (section_ids[None, :] == own_sections[:, None])
    scores = jnp.where(allowed[None, :, :], scores, jnp.float32(-1e30))
    probs = jax.nn.softmax(scores, axis=-1).astype(jnp.bfloat16)
    attended = jnp.einsum(
        "hqk,khd->qhd", probs, value_heads, preferred_element_type=jnp.float32
    ).astype(jnp.bfloat16)
    attended = attended.reshape(sections_here, local_heads * HEAD_DIM)
    head_terms = jnp.dot(attended, w_out, preferred_element_type=jnp.float32)
    combined = lax.psum(head_terms, "segment")
    return (section_in + combined).astype(jnp.bfloat16)


def solution(mesh):
    in_specs = (
        P("segment", "seq", None),
        P(),
        P(),
        P("seq"),
        P("seq", None),
        P(),
        P(None, "segment"),
        P(None, "segment"),
        P(None, "segment"),
        P("segment", None),
    )
    out_specs = P("seq", None)
    return jax.shard_map(shards, mesh=mesh, in_specs=in_specs, out_specs=out_specs, check_vma=False)
```

profile of v0, /device:TPU:0, one launch (start us, length us, event | category | flops | bytes accessed | tf_op | source)
XLA Modules:
  0.0 217.7 jit_solution(10877947771555918930)
XLA Ops:
  6.5 0.0 copy-start
  6.5 0.0 reduce-scatter.2.cloned.1.call-start
  6.5 0.9 fusion.30
  7.4 0.1 copy.25
  7.5 0.1 reduce-window.7
  7.6 0.1 reduce
  7.7 0.7 bitcast_subtract_fusion
  8.4 8.8 %fusion.3 = f32[64,8192]{1,0:T(8,128)S(1)} fusion(bf16[1,1024,8192]{2,1,0:T(8,128)(2,1)} %param.10, f32[64]{0:T(128)S(1)} %get-tuple-element.6, s32[1024]{0:T(1024)S(1)} %iota_add_fusion, s32[64]{0:T(128)S(1)} %reduce, s32[64]{0:T(128)S(1)} %bitcast_subtract_fusion), kind=kOutput, calls=%fused_computation.3 | convolution fusion | flops 1074462720 | bytes 18879232 | tf_op jit(solution)/shard_map/dot_general | solution.py:24
  17.3 0.0 copy-start.2
  17.3 0.0 copy-start.4
  17.3 0.0 copy-start.3
  17.3 1.8 fusion.25
  19.1 0.0 reduce-scatter.2.cloned.1.call-update
  19.1 0.0 all-reduce.5.cloned.1.call-start
  19.2 0.0 copy-done.2
  19.2 0.1 eq.52
  19.3 0.0 copy-done.4
  19.3 0.0 copy-done.3
  19.3 0.7 fusion.31
  20.6 0.2 dynamic-update-slice
  20.9 18.2 %all-reduce = bf16[32]{0:T(256)(128)(2,1)S(1)} all-reduce(bf16[32]{0:T(256)(128)(2,1)S(1)} %dynamic-update-slice), channel_id=1, replica_groups=mesh['segment'=4,'seq'=8] {'seq'}, use_global_device_ids=true, to_apply=%add | all-reduce | flops 32 | bytes 128
  39.1 0.1 convert_reduce_fusion
  39.2 15.9 %reduce-scatter.2.cloned.1.call-done = f32[32,1024]{1,0:T(8,128)} async-done(((f32[32,8192]{1,0:T(8,128)}), f32[32,1024]{1,0:T(8,128)}) %reduce-scatter.2.cloned.1.call-update) | async-done | bytes 131088 | tf_op jit(solution)/shard_map/reduce_scatter | solution.py:38
  55.1 0.0 all-reduce.5.cloned.1.call-update
  55.1 0.0 all-reduce.7.cloned.1.call-start
  55.8 0.0 copy-start.1
  55.8 42.1 %all-reduce.5.cloned.1.call-done = f32[32,1024]{1,0:T(8,128)} async-done(((f32[32,1024]{1,0:T(8,128)}), f32[32,1024]{1,0:T(8,128)}) %all-reduce.5.cloned.1.call-update) | async-done | bytes 131088 | tf_op jit(solution)/shard_map/psum | solution.py:39
  97.9 3.8 %fusion.20 = f32[32,2048]{1,0:T(8,128)} fusion(bf16[1024,2048]{1,0:T(8,128)(2,1)} %param.14, f32[32,1024]{1,0:T(8,128)} %all-reduce.5.cloned.1.call-done, f32[32]{0:T(128)S(1)} %broadcast_maximum_fusion), kind=kOutput, calls=%fused_computation.24 | convolution fusion | flops 134283264 | bytes 4587648 | tf_op jit(solution)/shard_map/dot_general | solution.py:41
  101.7 0.0 all-reduce.7.cloned.1.call-update
  101.7 0.1 fusion.29
  101.8 55.5 %all-reduce.7.cloned.1.call-done = f32[32,2048]{1,0:T(8,128)} async-done(((f32[32,2048]{1,0:T(8,128)}), f32[32,2048]{1,0:T(8,128)}) %all-reduce.7.cloned.1.call-update) | async-done | bytes 262160
  157.3 1.0 multiply_reduce_fusion
  158.3 0.0 copy-done.1
  158.3 2.0 fusion.11
  160.3 14.1 %all-gather.1 = bf16[8,4,512]{2,1,0:T(4,128)(2,1)S(1)} all-gather(bf16[1,4,512]{2,1,0:T(4,128)(2,1)S(1)} %fusion.11), channel_id=1, replica_groups=mesh['segment'=4,'seq'=8] {'seq'}, dimensions={0}, use_global_device_ids=true | all-gather | bytes 36864 | tf_op jit(solution)/shard_map/all_gather | solution.py:50
  174.4 2.2 fusion.8
  176.6 0.2 fusion.32
  176.8 2.1 fusion.9
  178.8 14.1 %all-gather = bf16[8,4,512]{2,1,0:T(4,128)(2,1)S(1)} all-gather(bf16[1,4,512]{2,1,0:T(4,128)(2,1)S(1)} %fusion.9), channel_id=1, replica_groups=mesh['segment'=4,'seq'=8] {'seq'}, dimensions={0}, use_global_device_ids=true | all-gather | bytes 36864 | tf_op jit(solution)/shard_map/all_gather | solution.py:51
  192.9 0.0 copy-done
  193.0 0.5 fusion.13
  193.5 16.2 %psum.15 = f32[4,2048]{1,0:T(4,128)S(1)} all-reduce(f32[4,2048]{1,0:T(4,128)S(1)} %fusion.13), channel_id=1, replica_groups=mesh['segment'=4,'seq'=8] {'segment'}, use_global_device_ids=true, to_apply=%region_8.9 | all-reduce | flops 8192 | bytes 65536 | tf_op jit(solution)/shard_map/psum | solution.py:68
  209.7 1.5 add_convert_fusion
  (9 shorter events, 0.1 us)
Async XLA Ops:
  6.5 186.4 %copy-start = (bf16[512,2048]{1,0:T(8,128)(2,1)S(1)}, bf16[512,2048]{1,0:T(8,128)(2,1)}, u32[]{:S(2)}) copy-start(bf16[512,2048]{1,0:T(8,128)(2,1)} %param.19) | copy-start | bytes 6291460
  6.5 48.5 %reduce-scatter.2.cloned.1.call-start = ((), (), s32[]{:S(2)}) async-start(), calls=%async_computation.1 | async-start | bytes 1179648 | tf_op jit(solution)/shard_map/reduce_scatter | solution.py:38
  17.3 1.9 copy-start.2
  17.3 2.0 copy-start.4
  17.3 2.0 copy-start.3
  19.1 78.7 %all-reduce.5.cloned.1.call-start = ((), (), s32[]{:S(2)}) async-start(), calls=%async_computation.2 | async-start | bytes 262144 | tf_op jit(solution)/shard_map/psum | solution.py:39
  55.1 102.2 %all-reduce.7.cloned.1.call-start = ((), (), s32[]{:S(2)}) async-start(), calls=%async_computation.3 | async-start | bytes 524288
  55.8 102.5 %copy-start.1 = (f32[2048]{0:T(1024)S(1)}, f32[2048]{0:T(1024)}, u32[]{:S(2)}) copy-start(f32[2048]{0:T(1024)} %param.15) | copy-start | bytes 24580
Sparse Core Ops, SparseCore 0:
  19.3 35.7 reduce-scatter.1
  58.0 39.8 all-reduce.4
  101.9 55.4 all-reduce.6
where the time goes:
time: 218 us
  waiting for transfers between devices  113 us (52%)
  blocking collectives  62.6 us (29%)
  matrix products  21.3 us (10%)
  between operations  14.5 us (7%)
  other arithmetic  4.58 us (2%)
    unnamed x4, waiting for transfers between devices  55.5 us
    psum x1, waiting for transfers between devices, shards(): doc_total = lax.psum(feature_block, 'segment')  42.1 us
    unnamed x1, blocking collectives  18.2 us
    psum x1, blocking collectives, shards(): combined = lax.psum(head_terms, 'segment')  16.2 us
    reduce_scatter x1, waiting for transfers between devices, shards(): lax.psum_scatter(section_part, 'seq', scatter_dimension=1, tiled=True)  15.9 us
    all_gather x1, blocking collectives, shards(): lax.all_gather(keys_here, 'seq', axis=0, tiled=True)  14.1 us
    all_gather x1, blocking collectives, shards(): lax.all_gather(values_here, 'seq', axis=0, tiled=True)  14.1 us
    dot_general x1, matrix products, shards(): partial_value = jnp.dot(member, tokens, preferred_element_type=jnp.float32)  8.85 us
  transfers between devices with their start and end apart: 3, of which 3 were waited for; matrix products, arithmetic and copies ran while one was open for 1% of the time, Pallas kernels for 0%

commit v1 on v0

--- a/solution.py
+++ b/solution.py
@@ -4,6 +4,9 @@
 from jax.sharding import PartitionSpec as P
 
 HEAD_DIM = 128
+settle_layers_all = lambda local_values: jnp.sum(
+    lax.all_gather(local_values, axis_name="segment"), axis=0
+)
 
 
 def shards(
@@ -36,7 +39,7 @@
     doc_onehot = (section_ids[:, None] == doc_sections[None, :]).astype(jnp.float32)
     section_part = jnp.dot(doc_onehot, weighted, precision=lax.Precision.HIGHEST)
     feature_block = lax.psum_scatter(section_part, "seq", scatter_dimension=1, tiled=True)
-    doc_total = lax.psum(feature_block, "segment")
+    doc_total = settle_layers_all(feature_block)
     pooled = (doc_total / jnp.maximum(count_all, 1.0)[:, None]).astype(jnp.bfloat16)
     projected = jnp.dot(pooled, w_in, preferred_element_type=jnp.float32)
     section_in = lax.psum_scatter(projected, "seq", scatter_dimension=0, tiled=True)

time: 218 us -> 183 us (0.84)
  waiting for transfers between devices: 113 us -> 67.9 us
  blocking collectives: 62.6 us -> 72.9 us
    psum x1 -> x0, waiting for transfers between devices: 42.1 us -> none  [shards(): doc_total = lax.psum(feature_block, 'segment')]
    all_gather x0 -> x1, blocking collectives: none -> 10.3 us  [lax.all_gather(local_values, axis_name='segment')]
    unnamed x4 -> x3, waiting for transfers between devices: 55.5 us -> 53.1 us
  transfers between devices with their start and end apart: 3 -> 2, of which waited for: 3 -> 2; matrix products, arithmetic and copies ran while one was open for 1% -> 1% of each run, Pallas kernels for 0% -> 0%
where the time goes in v1:
time: 183 us
  blocking collectives  72.9 us (40%)
  waiting for transfers between devices  67.9 us (37%)
  matrix products  21.3 us (12%)
  between operations  14.8 us (8%)
  other arithmetic  4.61 us (3%)
    unnamed x3, waiting for transfers between devices  53.1 us
    unnamed x1, blocking collectives  18.3 us
    psum x1, blocking collectives, shards(): combined = lax.psum(head_terms, 'segment')  16.2 us
    reduce_scatter x1, waiting for transfers between devices, shards(): lax.psum_scatter(section_part, 'seq', scatter_dimension=1, tiled=True)  14.7 us
    all_gather x1, blocking collectives, shards(): lax.all_gather(keys_here, 'seq', axis=0, tiled=True)  14.1 us
    all_gather x1, blocking collectives, shards(): lax.all_gather(values_here, 'seq', axis=0, tiled=True)  14.1 us
    all_gather x1, blocking collectives, lax.all_gather(local_values, axis_name='segment')  10.3 us
    dot_general x1, matrix products, shards(): partial_value = jnp.dot(member, tokens, preferred_element_type=jnp.float32)  8.85 us
  transfers between devices with their start and end apart: 2, of which 2 were waited for; matrix products, arithmetic and copies ran while one was open for 1% of the time, Pallas kernels for 0%

profile of v1, /device:TPU:0, one launch (start us, length us, event | category | flops | bytes accessed | tf_op | source)
XLA Modules:
  0.0 182.6 jit_solution(13610954959947405859)
XLA Ops:
  6.5 0.0 copy-start
  6.5 0.0 reduce-scatter.2.cloned.1.call-start
  6.5 0.9 fusion.30
  7.4 0.1 copy.25
  7.5 0.1 reduce-window.7
  7.6 0.1 reduce
  7.7 0.7 bitcast_subtract_fusion
  8.4 8.8 %fusion.3 = f32[64,8192]{1,0:T(8,128)S(1)} fusion(bf16[1,1024,8192]{2,1,0:T(8,128)(2,1)} %param.10, f32[64]{0:T(128)S(1)} %get-tuple-element.6, s32[1024]{0:T(1024)S(1)} %iota_add_fusion, s32[64]{0:T(128)S(1)} %reduce, s32[64]{0:T(128)S(1)} %bitcast_subtract_fusion), kind=kOutput, calls=%fused_computation.3 | convolution fusion | flops 1074462720 | bytes 18879232 | tf_op jit(solution)/shard_map/dot_general | solution.py:27
  17.3 0.0 copy-start.2
  17.3 0.0 copy-start.4
  17.3 0.0 copy-start.3
  17.3 1.8 %fusion.25 = f32[32,8192]{1,0:T(8,128)} fusion(f32[64,8192]{1,0:T(8,128)S(1)} %fusion.3, s32[64]{0:T(128)S(1)} %get-tuple-element.9), kind=kOutput, calls=%fused_computation.34 | convolution fusion | flops 201328640 | bytes 3145984 | tf_op jit(solution)/shard_map/dot_general | solution.py:40
  19.1 0.0 reduce-scatter.2.cloned.1.call-update
  19.1 0.0 all-reduce.4.cloned.1.call-start
  19.2 0.0 copy-done.2
  19.2 0.1 eq.52
  19.3 0.0 copy-done.4
  19.3 0.0 copy-done.3
  19.3 0.7 fusion.31
  21.2 0.2 dynamic-update-slice
  21.5 18.3 %all-reduce = bf16[32]{0:T(256)(128)(2,1)S(1)} all-reduce(bf16[32]{0:T(256)(128)(2,1)S(1)} %dynamic-update-slice), channel_id=1, replica_groups=mesh['segment'=4,'seq'=8] {'seq'}, use_global_device_ids=true, to_apply=%add | all-reduce | flops 32 | bytes 128
  39.7 0.1 convert_reduce_fusion
  39.9 14.7 %reduce-scatter.2.cloned.1.call-done = f32[32,1024]{1,0:T(8,128)} async-done(((f32[32,8192]{1,0:T(8,128)}), f32[32,1024]{1,0:T(8,128)}) %reduce-scatter.2.cloned.1.call-update) | async-done | bytes 131088 | tf_op jit(solution)/shard_map/reduce_scatter | solution.py:41
  54.6 10.3 %all-gather = f32[128,1024]{1,0:T(8,128)S(1)} all-gather(f32[32,1024]{1,0:T(8,128)} %reduce-scatter.2.cloned.1.call-done), channel_id=2, replica_groups=mesh['segment'=4,'seq'=8] {'segment'}, dimensions={0}, use_global_device_ids=true | all-gather | bytes 655360 | tf_op jit(solution)/shard_map/all_gather | solution.py:8
  64.9 0.0 copy-start.1
  64.9 3.8 %fusion.20 = f32[32,2048]{1,0:T(8,128)} fusion(bf16[1024,2048]{1,0:T(8,128)(2,1)} %param.14, f32[32,1024]{1,0:T(8,128)S(1)} %reduce_sum.36, f32[32]{0:T(128)S(1)} %broadcast_maximum_fusion), kind=kOutput, calls=%fused_computation.24 | convolution fusion | flops 134283264 | bytes 4587648 | tf_op jit(solution)/shard_map/dot_general | solution.py:44
  68.7 0.0 all-reduce.4.cloned.1.call-update
  68.7 0.1 fusion.29
  68.8 53.1 %all-reduce.4.cloned.1.call-done = f32[32,2048]{1,0:T(8,128)} async-done(((f32[32,2048]{1,0:T(8,128)}), f32[32,2048]{1,0:T(8,128)}) %all-reduce.4.cloned.1.call-update) | async-done | bytes 262160
  121.9 1.0 multiply_reduce_fusion
  122.9 0.0 copy-done.1
  122.9 2.0 %fusion.11 = bf16[1,4,512]{2,1,0:T(4,128)(2,1)S(1)} fusion(bf16[2048,512]{1,0:T(8,128)(2,1)} %param.17, f32[32,2048]{1,0:T(8,128)} %all-reduce.4.cloned.1.call-done, u32[]{:T(128)S(6)} %multiply.11, f32[2048]{0:T(1024)S(1)} %copy-done.1, f32[4]{0:T(128)S(1)} %add_rsqrt_fusion), kind=kOutput, calls=%fused_computation.14 | convolution fusion | flops 8415232 | bytes 2142228 | tf_op jit(solution)/shard_map/dot_general | solution.py:49
  125.0 14.1 %all-gather.2 = bf16[8,4,512]{2,1,0:T(4,128)(2,1)S(1)} all-gather(bf16[1,4,512]{2,1,0:T(4,128)(2,1)S(1)} %fusion.11), channel_id=1, replica_groups=mesh['segment'=4,'seq'=8] {'seq'}, dimensions={0}, use_global_device_ids=true | all-gather | bytes 36864 | tf_op jit(solution)/shard_map/all_gather | solution.py:53
  139.1 2.2 %fusion.8 = f32[4,4,32]{2,1,0:T(4,128)S(1)} fusion(bf16[2048,512]{1,0:T(8,128)(2,1)} %param.16, bf16[32,4,128]{2,1,0:T(4,128)(2,1)S(1)} %reshape.108, pred[4,32]{1,0:T(4,128)(4,1)S(1)} %fusion.29, f32[32,2048]{1,0:T(8,128)} %all-reduce.4.cloned.1.call-done, u32[]{:T(128)S(6)} %multiply.11, f32[2048]{0:T(1024)S(1)} %copy-done.1, f32[4]{0:T(128)S(1)} %add_rsqrt_fusion), kind=kOutput, calls=%fused_computation.7 | convolution fusion | flops 8547328 | bytes 2173076 | tf_op jit(solution)/shard_map/qhd,khd->hqk/dot_general | solution.py:61
  141.2 0.2 fusion.32
  141.4 2.1 %fusion.9 = bf16[1,4,512]{2,1,0:T(4,128)(2,1)S(1)} fusion(bf16[2048,512]{1,0:T(8,128)(2,1)} %param.18, f32[32,2048]{1,0:T(8,128)} %all-reduce.4.cloned.1.call-done, u32[]{:T(128)S(6)} %multiply.11, f32[2048]{0:T(1024)S(1)} %copy-done.1, f32[4]{0:T(128)S(1)} %add_rsqrt_fusion), kind=kOutput, calls=%fused_computation.12 | convolution fusion | flops 8415232 | bytes 2142228 | tf_op jit(solution)/shard_map/dot_general | solution.py:50
  143.5 14.1 %all-gather.1 = bf16[8,4,512]{2,1,0:T(4,128)(2,1)S(1)} all-gather(bf16[1,4,512]{2,1,0:T(4,128)(2,1)S(1)} %fusion.9), channel_id=1, replica_groups=mesh['segment'=4,'seq'=8] {'seq'}, dimensions={0}, use_global_device_ids=true | all-gather | bytes 36864 | tf_op jit(solution)/shard_map/all_gather | solution.py:54
  157.6 0.0 copy-done
  157.6 0.5 fusion.13
  158.1 16.2 %psum.7 = f32[4,2048]{1,0:T(4,128)S(1)} all-reduce(f32[4,2048]{1,0:T(4,128)S(1)} %fusion.13), channel_id=1, replica_groups=mesh['segment'=4,'seq'=8] {'segment'}, use_global_device_ids=true, to_apply=%region_8.9 | all-reduce | flops 8192 | bytes 65536 | tf_op jit(solution)/shard_map/psum | solution.py:71
  174.3 1.5 add_convert_fusion
  (10 shorter events, 0.1 us)
Async XLA Ops:
  6.5 151.0 %copy-start = (bf16[512,2048]{1,0:T(8,128)(2,1)S(1)}, bf16[512,2048]{1,0:T(8,128)(2,1)}, u32[]{:S(2)}) copy-start(bf16[512,2048]{1,0:T(8,128)(2,1)} %param.19) | copy-start | bytes 6291460
  6.5 48.1 %reduce-scatter.2.cloned.1.call-start = ((), (), s32[]{:S(2)}) async-start(), calls=%async_computation.1 | async-start | bytes 1179648 | tf_op jit(solution)/shard_map/reduce_scatter | solution.py:41
  17.3 1.9 %copy-start.2 = (s32[4,64]{1,0:T(4,128)S(1)}, s32[4,64]{1,0:T(4,128)}, u32[]{:S(2)}) copy-start(s32[4,64]{1,0:T(4,128)} %param.12) | copy-start | bytes 3076
  17.3 2.0 %copy-start.4 = (s32[4]{0:T(128)S(1)}, s32[4]{0:T(128)}, u32[]{:S(2)}) copy-start(s32[4]{0:T(128)} %param.13) | copy-start | bytes 52
  17.3 2.0 %copy-start.3 = (u32[32]{0:T(128)S(1)}, u32[32]{0:T(128)}, u32[]{:S(2)}) copy-start(u32[32]{0:T(128)} %constant.45) | copy-start | bytes 388
  19.1 102.8 %all-reduce.4.cloned.1.call-start = ((), (), s32[]{:S(2)}) async-start(), calls=%async_computation.2 | async-start | bytes 524288
  64.9 58.0 %copy-start.1 = (f32[2048]{0:T(1024)S(1)}, f32[2048]{0:T(1024)}, u32[]{:S(2)}) copy-start(f32[2048]{0:T(1024)} %param.15) | copy-start | bytes 24580
Sparse Core Ops, SparseCore 0:
  19.3 35.2 reduce-scatter.1
  68.9 53.0 all-reduce.3
